TPU v7x, 128 devices: a whole 4x4x4 slice. The times are simulated.
128 devices in a mesh: ctx: 16 (over z, x), tp: 8 (over y, core).
Axes of the slice: x: 4, y: 4, z: 4, core: 2. Of those that a mesh axis runs over, the one named last changes fastest.
Arguments:
- projected: bfloat16 [3, 8192, 8192], P(None, 'ctx', 'tp'), may hold values from -6 to 6
- short_filter: float32 [3, 3, 8192], P(None, None, 'tp'), may hold values from -3.5 to 3.5
- long_filter: bfloat16 [128, 8192], P(None, 'tp'), may hold values from -0.5 to 0.5
- skip_gain: float32 [8192], P('tp'), may hold values from -3 to 3
- out_weight: bfloat16 [8192, 8192], P('tp', 'ctx'), may hold values from -0.0625 to 0.0625
- out_grad: bfloat16 [8192, 8192], P('ctx'), may hold values from -6 to 6
- left_source: int32 [16], replicated, may hold values from -1 to 15, as said below
Outputs:
- mixed: bfloat16 [8192, 8192], P(('ctx', 'tp'))
- grad_projected: bfloat16 [3, 8192, 8192], P(None, 'ctx', 'tp')
- grad_long: float32 [128, 8192], P(None, 'tp')
- grad_short: float32 [3, 3, 8192], P(None, None, 'tp')
Inputs may be any that keep to these rules, and one draw needn't show every extreme that they name: left_source[b] is -1 where block b begins a contig, else another block; no block is named by two blocks, and following left_source from any block ends at -1 without repeating a block.
All inputs are finite; a program needn't handle non-finite values.
Results may differ from a plain program's by a relative error of at most 0.015.
Values may be sent and summed in bfloat16 or wider, within the bound.
No kernel may reach another device: no remote copies, remote signals or barrier semaphores. Data moves between devices by JAX's collectives and lax.ppermute only.
A program may use at most 128 MiB of HBM per device.

v0:
```python
import math
import jax
import jax.numpy as jnp
from jax import lax
from jax.sharding import PartitionSpec as P

edge_depth = 8


def short_forward(extended, tap_weights, out_rows):
    summed = jnp.zeros((extended.shape[0], out_rows, extended.shape[2]), jnp.float32)
    for shift in range(tap_weights.shape[1]):
        piece = extended[:, edge_depth - shift : edge_depth - shift + out_rows].astype(jnp.float32)
        summed = summed + tap_weights[:, shift][:, None, :] * piece
    return summed


def depthwise(signal, kernel):
    channels = signal.shape[1]
    result = lax.conv_general_dilated(
        signal[None],
        kernel[:, None, :],
        (1,),
        "VALID",
        dimension_numbers=("NWC", "WIO", "NWC"),
        feature_group_count=channels,
        preferred_element_type=jnp.float32,
    )
    return result[0]


def causal_conv(extended, flipped_taps):
    return depthwise(extended[1:], flipped_taps)


def lag_sums(grad_conv, extended):
    return jnp.flip(depthwise(extended[1:], grad_conv), 0)


def select_slot(stacked, slot, live):
    picked = lax.dynamic_index_in_dim(stacked, slot, 0, keepdims=False)
    return jnp.where(live, picked, jnp.zeros_like(picked))


def on_device(projected, short_filter, long_filter, skip_gain, out_weight, out_grad, left_source):
    rows_here = projected.shape[1]
    filt_len = long_filter.shape[0]
    ctx_count = lax.axis_size("ctx")
    my_index = lax.axis_index("ctx")
    positions = jnp.arange(ctx_count, dtype=jnp.int32)
    source_raw = left_source[my_index]
    has_left = source_raw >= 0
    source = jnp.maximum(source_raw, 0)
    is_reader = left_source == my_index
    has_right = jnp.any(is_reader)
    reader = jnp.sum(jnp.where(is_reader, positions, 0))
    flipped_taps = jnp.flip(long_filter, 0)
    skip_row = skip_gain[None, :]
    act_rest = short_forward(projected, short_filter, rows_here - edge_depth)
    mixin_rest = (act_rest[1] * act_rest[2]).astype(jnp.bfloat16)
    raw_tail = projected[:, rows_here - edge_depth :]
    mixin_tail = mixin_rest[mixin_rest.shape[0] - filt_len :]
    slot_mark = ((positions == reader) & has_right).astype(jnp.bfloat16)
    sent_raw = slot_mark[:, None, None, None] * raw_tail[None]
    sent_mixin = slot_mark[:, None, None] * mixin_tail[None]
    got_raw, got_mixin = (
        lax.all_to_all(sent_raw, "ctx", split_axis=0, concat_axis=0, tiled=True),
        lax.all_to_all(sent_mixin, "ctx", split_axis=0, concat_axis=0, tiled=True),
    )
    left_raw = select_slot(got_raw, source, has_left)
    left_mixin = select_slot(got_mixin, source, has_left)
    streams_ext = jnp.concatenate([left_raw, projected], 1)
    act_head = short_forward(streams_ext[:, : 2 * edge_depth], short_filter, edge_depth)
    act = jnp.concatenate([act_head, act_rest], 1)
    mixin_head = (act_head[1] * act_head[2]).astype(jnp.bfloat16)
    mixin = jnp.concatenate([mixin_head, mixin_rest], 0)
    mixin_ext = jnp.concatenate([left_mixin, mixin], 0)
    conv = causal_conv(mixin_ext, flipped_taps)
    conv = conv + skip_row * mixin.astype(jnp.float32)
    gated = (act[0] * conv).astype(jnp.bfloat16)
    full_weight = lax.all_gather(out_weight, "ctx", axis=1, tiled=True)
    share_rows = rows_here // lax.axis_size("tp")
    gated_rows = lax.slice_in_dim(gated, 0, lax.axis_size("tp") * share_rows, axis=0)
    mixed = lax.psum_scatter(
        jnp.dot(gated_rows, full_weight, preferred_element_type=jnp.float32).astype(jnp.bfloat16),
        "tp",
        scatter_dimension=0,
        tiled=True,
    )
    back_grad = lax.dot_general(
        out_grad, full_weight, (((1,), (1,)), ((), ())), preferred_element_type=jnp.float32
    )
    grad_conv = (back_grad * act[0]).astype(jnp.bfloat16)
    grad_gate = back_grad * conv
    flipped = jnp.flip(grad_conv, 0)
    back_mark = ((positions == source) & has_left).astype(jnp.bfloat16)
    sent_head = back_mark[:, None, None] * grad_conv[None, :filt_len]
    got_head = lax.all_to_all(sent_head, "ctx", split_axis=0, concat_axis=0, tiled=True)
    right_head = select_slot(got_head, reader, has_right)
    flipped_ext = jnp.concatenate([jnp.flip(right_head, 0), flipped], 0)
    flipped_conv = causal_conv(flipped_ext, flipped_taps)
    grad_wide = grad_conv.astype(jnp.float32)
    grad_mixin = jnp.flip(flipped_conv, 0) + skip_row * grad_wide
    grad_act = jnp.stack([grad_gate, grad_mixin * act[2], grad_mixin * act[1]])
    wide_mark = back_mark.astype(jnp.float32)
    sent_rows = wide_mark[:, None, None, None] * grad_act[None, :, :edge_depth]
    got_rows = lax.all_to_all(
        sent_rows.astype(jnp.bfloat16), "ctx", split_axis=0, concat_axis=0, tiled=True
    ).astype(sent_rows.dtype)
    right_rows = select_slot(got_rows, reader, has_right)
    grad_act_ext = jnp.concatenate([grad_act, right_rows], 1)
    grad_streams = jnp.zeros(grad_act.shape, jnp.float32)
    for shift in range(short_filter.shape[1]):
        grad_streams = (
            grad_streams
            + short_filter[:, shift][:, None, :] * grad_act_ext[:, shift : shift + rows_here]
        )
    short_terms = jnp.stack(
        [
            jnp.sum(
                grad_act
                * streams_ext[:, edge_depth - shift : edge_depth - shift + rows_here].astype(
                    jnp.float32
                ),
                axis=1,
            )
            for shift in range(short_filter.shape[1])
        ],
        axis=1,
    )
    long_terms = lag_sums(grad_conv, mixin_ext)
    long_total, short_total = (
        lax.psum(long_terms.astype(jnp.bfloat16), "ctx").astype(jnp.float32),
        lax.psum(short_terms.astype(jnp.bfloat16), "ctx").astype(jnp.float32),
    )
    grad_scale = 1.0 / math.sqrt(rows_here * ctx_count)
    return (
        mixed,
        grad_streams.astype(jnp.bfloat16),
        long_total * grad_scale,
        short_total * grad_scale,
    )


def solution(mesh):
    placed = (
        P(None, "ctx", "tp"),
        P(None, None, "tp"),
        P(None, "tp"),
        P("tp"),
        P("tp", "ctx"),
        P("ctx", None),
        P(),
    )
    return jax.shard_map(
        on_device,
        mesh=mesh,
        in_specs=placed,
        out_specs=(
            P(("ctx", "tp"), None),
            P(None, "ctx", "tp"),
            P(None, "tp"),
            P(None, None, "tp"),
        ),
        check_vma=False,
    )
```

profile of v0, /device:TPU:24, one launch (start us, length us, event | category | flops | bytes accessed | tf_op | source)
XLA Modules:
  0.0 475.2 jit_solution(3345166502420664161)
XLA Ops:
  13.8 7.9 %all-to-all-start = ((bf16[16,3,8,1024]{3,2,1,0:T(8,128)(2,1)}), bf16[16,3,8,1024]{3,2,1,0:T(8,128)(2,1)}, u32[]{:S(2)}, u32[]{:S(2)}) async-start(bf16[16,3,8,1024]{3,2,1,0:T(8,128)(2,1)} %broadcast_multiply_fusion.2), calls=%async_computation | async-start | bytes 1572864 | tf_op jit(solution)/shard_map/all_to_all | solution.py:67
  24.1 2.7 copy-done.2
  29.4 12.3 %all-to-all-done = bf16[16,3,8,1024]{3,2,1,0:T(8,128)(2,1)} async-done(((bf16[16,3,8,1024]{3,2,1,0:T(8,128)(2,1)}), bf16[16,3,8,1024]{3,2,1,0:T(8,128)(2,1)}, u32[]{:S(2)}, u32[]{:S(2)}) %all-to-all-start) | async-done | bytes 786464 | tf_op jit(solution)/shard_map/all_to_all | solution.py:67
  41.7 4.5 all-to-all-start.1
  48.2 2.8 rev.19
  51.0 3.5 fusion.36
  56.0 66.2 %all-to-all-done.1 = bf16[16,128,1024]{2,1,0:T(8,128)(2,1)} async-done(((bf16[16,128,1024]{2,1,0:T(8,128)(2,1)}), bf16[16,128,1024]{2,1,0:T(8,128)(2,1)}, u32[]{:S(2)}, u32[]{:S(2)}) %all-to-all-start.1) | async-done | bytes 4194336 | tf_op jit(solution)/shard_map/all_to_all | solution.py:68
  125.8 32.3 %fusion.19 = f32[1,512,1024]{2,0,1:T(1,128)} fusion(bf16[1,639,1024]{2,1,0:T(8,128)(2,1)S(1)} %fusion.22, bf16[128,1,1024]{2,0,1:T(8,128)(2,1)S(1)} %bitcast.82), kind=kOutput, calls=%fused_computation.45 | convolution fusion | flops 134217728 | bytes 3667968 | tf_op jit(solution)/shard_map/conv_general_dilated | solution.py:20
  158.1 23.1 %all-gather.2.cloned.1.call-done = bf16[1024,8192]{1,0:T(8,128)(2,1)} async-done(((bf16[1024,512]{1,0:T(8,128)(2,1)}), bf16[1024,8192]{1,0:T(8,128)(2,1)}) %all-gather.2.cloned.1.call-update) | async-done | bytes 16777232 | tf_op jit(solution)/shard_map/all_gather | solution.py:81
  181.2 16.8 %multiply_bitcast_fusion = (f32[1,512,1024]{2,1,0:T(8,128)}, bf16[512,1024]{1,0:T(8,128)(2,1)S(1)}) fusion(f32[1,512,1024]{2,0,1:T(1,128)} %fusion.19, f32[1024]{0:T(1024)S(1)} %copy-done.20, bf16[504,1024]{1,0:T(8,128)(2,1)S(1)} %copy-done.7, bf16[8,1024]{1,0:T(8,128)(2,1)S(1)} %fusion.27, f32[3,504,1024]{2,1,0:T(8,128)} %copy-done.2, ...), kind=kOutput, calls=%fused_computation.39 | convolution fusion | flops 8595177472 | bytes 37752832 | tf_op jit(solution)/shard_map/dot_general | solution.py:90
  198.0 28.3 %fusion.15 = bf16[1,128,1024]{2,0,1:T(2,128)(2,1)S(1)} fusion(bf16[512,1,1024]{2,0,1:T(8,128)(2,1)S(1)} %bitcast.80, bf16[1,639,1024]{2,1,0:T(8,128)(2,1)} %copy-done.8), kind=kOutput, calls=%fused_computation.34 | convolution fusion | flops 134217728 | bytes 2619392 | tf_op jit(solution)/shard_map/conv_general_dilated | solution.py:20
  226.4 2.6 rev.23
  229.0 17.8 %convolution_convert_fusion = bf16[512,8192]{1,0:T(8,128)(2,1)} fusion(bf16[1024,8192]{1,0:T(8,128)(2,1)} %all-gather.2.cloned.1.call-done, f32[1,512,1024]{2,0,1:T(1,128)} %fusion.19, f32[1024]{0:T(1024)S(1)} %copy-done.20, bf16[504,1024]{1,0:T(8,128)(2,1)S(1)} %copy-done.7, bf16[8,1024]{1,0:T(8,128)(2,1)S(1)} %fusion.27, f32[3,504,1024]{2,1,0:T(8,128)} %copy-done.2, ...), kind=kOutput, calls=%fused_computation | convolution fusion | flops 8598847488 | bytes 34607104 | tf_op jit(solution)/shard_map/dot_general | solution.py:85
  246.9 2.4 broadcast_multiply_fusion
  249.3 7.8 %all-to-all-start.2 = ((bf16[16,128,1024]{2,1,0:T(8,128)(2,1)}), bf16[16,128,1024]{2,1,0:T(8,128)(2,1)}, u32[]{:S(2)}, u32[]{:S(2)}) async-start(bf16[16,128,1024]{2,1,0:T(8,128)(2,1)} %broadcast_multiply_fusion), calls=%async_computation.3 | async-start | bytes 8388608 | tf_op jit(solution)/shard_map/all_to_all | solution.py:98
  260.3 58.0 %all-to-all-done.2 = bf16[16,128,1024]{2,1,0:T(8,128)(2,1)} async-done(((bf16[16,128,1024]{2,1,0:T(8,128)(2,1)}), bf16[16,128,1024]{2,1,0:T(8,128)(2,1)}, u32[]{:S(2)}, u32[]{:S(2)}) %all-to-all-start.2) | async-done | bytes 4194336 | tf_op jit(solution)/shard_map/all_to_all | solution.py:98
  320.5 31.7 %fusion.4 = f32[1,512,1024]{2,0,1:T(1,128)S(1)} fusion(bf16[1,639,1024]{2,1,0:T(8,128)(2,1)S(1)} %fusion.21, bf16[128,1,1024]{2,0,1:T(8,128)(2,1)S(1)} %bitcast.83), kind=kOutput, calls=%fused_computation.20 | convolution fusion | flops 134217728 | bytes 3667968 | tf_op jit(solution)/shard_map/conv_general_dilated | solution.py:20
  352.7 10.3 %rev.22 = f32[512,1024]{1,0:T(8,128)} reverse(f32[512,1024]{1,0:T(8,128)S(1)} %bitcast.79), dimensions={0} | reverse | bytes 4194304 | tf_op jit(solution)/shard_map/jit(_flip)/rev | solution.py:103
  363.0 3.9 fusion.9
  369.8 4.0 all-to-all-start.3
  375.6 10.8 %all-to-all-done.3 = bf16[16,3,8,1024]{3,2,1,0:T(8,128)(2,1)S(1)} async-done(((bf16[16,3,8,1024]{3,2,1,0:T(8,128)(2,1)}), bf16[16,3,8,1024]{3,2,1,0:T(8,128)(2,1)S(1)}, u32[]{:S(2)}, u32[]{:S(2)}) %all-to-all-start.3) | async-done | bytes 786464 | tf_op jit(solution)/shard_map/all_to_all | solution.py:107
  387.1 2.8 pad_maximum_fusion
  391.8 5.6 %multiply_reduce_fusion.1 = (bf16[3,1024]{1,0:T(4,128)(2,1)S(1)}, bf16[3,1024]{1,0:T(4,128)(2,1)S(1)}, bf16[3,1024]{1,0:T(4,128)(2,1)S(1)}, bf16[3,512,1024]{2,1,0:T(8,128)(2,1)}) fusion(bf16[3,8,1024]{2,1,0:T(8,128)(2,1)S(1)} %copy-done.10, bf16[3,512,1024]{2,1,0:T(8,128)(2,1)S(1)} %copy-done.1, f32[1,512,1024]{2,1,0:T(8,128)S(1)} %copy-done.4, ...), kind=kLoop, calls=%fused_computation.11 | loop fusion | flops 36166656 | bytes 25270272 | tf_op jit(solution)/shard_map/reduce_sum | solution.py:120
  397.4 70.6 %psum.15 = bf16[3,3,1024]{2,0,1:T(4,128)(2,1)S(1)} all-reduce(bf16[3,3,1024]{2,0,1:T(4,128)(2,1)S(1)} %pad_maximum_fusion.9), channel_id=1, replica_groups=mesh['ctx'=16,'tp'=8] {'ctx'}, use_global_device_ids=true, to_apply=%region_7.8 | all-reduce | flops 9216 | bytes 36864 | tf_op jit(solution)/shard_map/psum | solution.py:134
  (85 shorter events, 29.2 us)
Async XLA Ops:
  7.2 14.7 %copy-start = (bf16[3,512,1024]{2,1,0:T(8,128)(2,1)S(1)}, bf16[3,512,1024]{2,1,0:T(8,128)(2,1)}, u32[]{:S(2)}) copy-start(bf16[3,512,1024]{2,1,0:T(8,128)(2,1)} %param.7) | copy-start | bytes 9437188
  7.2 14.5 %copy-start.19 = (f32[3,3,1024]{2,1,0:T(4,128)S(1)}, f32[3,3,1024]{2,1,0:T(4,128)}, u32[]{:S(2)}) copy-start(f32[3,3,1024]{2,1,0:T(4,128)} %param.8) | copy-start | bytes 110596
  7.2 174.1 %all-gather.2.cloned.1.call-start = ((), (), s32[]{:S(2)}) async-start(), calls=%async_computation.5 | async-start | bytes 17825792 | tf_op jit(solution)/shard_map/all_gather | solution.py:81
  13.8 28.0 %all-to-all-start = ((bf16[16,3,8,1024]{3,2,1,0:T(8,128)(2,1)}), bf16[16,3,8,1024]{3,2,1,0:T(8,128)(2,1)}, u32[]{:S(2)}, u32[]{:S(2)}) async-start(bf16[16,3,8,1024]{3,2,1,0:T(8,128)(2,1)} %broadcast_multiply_fusion.2), calls=%async_computation | async-start | bytes 1572864 | tf_op jit(solution)/shard_map/all_to_all | solution.py:67
  21.8 33.6 %copy-start.13 = (f32[3,1,1024]{2,0,1:T(4,128)}, f32[3,1,1024]{2,0,1:T(4,128)S(1)}, u32[]{:S(2)}) copy-start(f32[3,1,1024]{2,0,1:T(4,128)S(1)} %copy.53) | copy-start | bytes 36868
  21.8 33.5 %copy-start.15 = (f32[3,1024]{1,0:T(4,128)}, f32[3,1024]{1,0:T(4,128)S(1)}, u32[]{:S(2)}) copy-start(f32[3,1024]{1,0:T(4,128)S(1)} %get-tuple-element.21) | copy-start | bytes 36868
  21.8 33.5 %copy-start.17 = (f32[3,1024]{1,0:T(4,128)}, f32[3,1024]{1,0:T(4,128)S(1)}, u32[]{:S(2)}) copy-start(f32[3,1024]{1,0:T(4,128)S(1)} %get-tuple-element.22) | copy-start | bytes 36868
  29.4 16.9 %copy-start.21 = (s32[16]{0:T(128)S(1)}, s32[16]{0:T(128)}, u32[]{:S(2)}) copy-start(s32[16]{0:T(128)} %param.13) | copy-start | bytes 196
  29.4 18.8 %copy-start.11 = (bf16[128,1024]{1,0:T(8,128)(2,1)S(1)}, bf16[128,1024]{1,0:T(8,128)(2,1)}, u32[]{:S(2)}) copy-start(bf16[128,1024]{1,0:T(8,128)(2,1)} %param.9) | copy-start | bytes 786436
  41.7 80.4 %all-to-all-start.1 = ((bf16[16,128,1024]{2,1,0:T(8,128)(2,1)}), bf16[16,128,1024]{2,1,0:T(8,128)(2,1)}, u32[]{:S(2)}, u32[]{:S(2)}) async-start(bf16[16,128,1024]{2,1,0:T(8,128)(2,1)} %broadcast_multiply_fusion.1), calls=%async_computation.1 | async-start | bytes 8388608 | tf_op jit(solution)/shard_map/all_to_all | solution.py:68
  46.3 327.5 %all-reduce.2.cloned.1.call-start = ((), (), s32[]{:S(2)}) async-start(), calls=%async_computation.7 | async-start | bytes 524288 | tf_op jit(solution)/shard_map/psum | solution.py:133
  55.4 70.4 %copy-start.12 = (bf16[128,1024]{1,0:T(8,128)(2,1)S(1)}, bf16[128,1024]{1,0:T(8,128)(2,1)}, u32[]{:S(2)}) copy-start(bf16[128,1024]{1,0:T(8,128)(2,1)} %rev.19) | copy-start | bytes 786436
  125.8 55.4 %copy-start.7 = (bf16[504,1024]{1,0:T(8,128)(2,1)S(1)}, bf16[504,1024]{1,0:T(8,128)(2,1)}, u32[]{:S(2)}) copy-start(bf16[504,1024]{1,0:T(8,128)(2,1)} %fusion.36) | copy-start | bytes 3096580
  125.8 55.4 %copy-start.20 = (f32[1024]{0:T(1024)S(1)}, f32[1024]{0:T(1024)}, u32[]{:S(2)}) copy-start(f32[1024]{0:T(1024)} %param.10) | copy-start | bytes 12292
  229.0 239.7 %reduce-scatter.2.cloned.1.call-start = ((), (), s32[]{:S(2)}) async-start(), calls=%async_computation.6 | async-start | bytes 9437184 | tf_op jit(solution)/shard_map/reduce_scatter | solution.py:84
  249.3 69.0 %all-to-all-start.2 = ((bf16[16,128,1024]{2,1,0:T(8,128)(2,1)}), bf16[16,128,1024]{2,1,0:T(8,128)(2,1)}, u32[]{:S(2)}, u32[]{:S(2)}) async-start(bf16[16,128,1024]{2,1,0:T(8,128)(2,1)} %broadcast_multiply_fusion), calls=%async_computation.3 | async-start | bytes 8388608 | tf_op jit(solution)/shard_map/all_to_all | solution.py:98
  363.0 4.0 copy-start.5
  369.8 16.6 %all-to-all-start.3 = ((bf16[16,3,8,1024]{3,2,1,0:T(8,128)(2,1)}), bf16[16,3,8,1024]{3,2,1,0:T(8,128)(2,1)S(1)}, u32[]{:S(2)}, u32[]{:S(2)}) async-start(bf16[16,3,8,1024]{3,2,1,0:T(8,128)(2,1)} %multiply_convert_fusion.2), calls=%async_computation.4 | async-start | bytes 1572864 | tf_op jit(solution)/shard_map/all_to_all | solution.py:107
  387.1 4.0 copy-start.4
  387.1 4.7 copy-start.6
  387.1 4.6 copy-start.10
  387.1 4.6 copy-start.14
  387.1 4.6 copy-start.16
  387.1 4.6 copy-start.18
  (5 other events, 9.4 us)
Sparse Core Ops, SparseCore 0:
  10.1 171.0 all-gather.1
  229.1 118.2 all-reduce.1
  350.4 49.8 reduce-scatter.1
where the time goes:
time: 476 us; the launch traced here: 475 us
  waiting for transfers between devices  171 us (36%)
  matrix products  127 us (27%)
  blocking collectives  70.6 us (15%)
  other arithmetic  37.8 us (8%)
  local copies, waits for them, and re-layouts  27 us (6%)
  starting transfers between devices  24.4 us (5%)
  between operations  17.3 us (4%)
    conv_general_dilated x3, matrix products, depthwise(): lax.conv_general_dilated(signal[None], kernel[:, None, :], (1,), 'VALID',...  92.3 us
    psum x1, blocking collectives, on_device(): lax.psum(short_terms.astype(jnp.bfloat16), 'ctx').astype(jnp.float32)  70.6 us
    all_to_all x1, waiting for transfers between devices, on_device(): lax.all_to_all(sent_mixin, 'ctx', split_axis=0, concat_axis=0, tiled=True)  66.2 us
    all_to_all x1, waiting for transfers between devices, on_device(): lax.all_to_all(sent_head, 'ctx', split_axis=0, concat_axis=0, tiled=True)  58 us
    all_gather x1, waiting for transfers between devices, on_device(): full_weight = lax.all_gather(out_weight, 'ctx', axis=1, tiled=True)  23.1 us
    dot_general x1, matrix products, on_device(): jnp.dot(gated_rows, full_weight, preferred_element_type=jnp.float32)  17.8 us
    dot_general x1, matrix products, on_device(): lax.dot_general(out_grad, full_weight, (((1,), (1,)), ((), ())), preferre...  16.8 us
    all_to_all x1, waiting for transfers between devices, on_device(): lax.all_to_all(sent_raw, 'ctx', split_axis=0, concat_axis=0, tiled=True)  12.3 us
  transfers between devices with their start and end apart: 7, of which 5 were waited for; matrix products, arithmetic and copies ran while one was open for 29% of the time, Pallas kernels for 0%

commit v1 on v0

--- a/solution.py
+++ b/solution.py
@@ -5,6 +5,11 @@
 from jax.sharding import PartitionSpec as P
 
 edge_depth = 8
+
+
+def add_all(x, axis):
+    blocks = lax.all_gather(x, axis)
+    return jnp.sum(blocks, axis=0)
 
 
 def short_forward(extended, tap_weights, out_rows):
@@ -131,7 +136,7 @@
     long_terms = lag_sums(grad_conv, mixin_ext)
     long_total, short_total = (
         lax.psum(long_terms.astype(jnp.bfloat16), "ctx").astype(jnp.float32),
-        lax.psum(short_terms.astype(jnp.bfloat16), "ctx").astype(jnp.float32),
+        add_all(short_terms.astype(jnp.bfloat16), "ctx").astype(jnp.float32),
     )
     grad_scale = 1.0 / math.sqrt(rows_here * ctx_count)
     return (

time: 476 us -> 427 us (0.90)
  blocking collectives: 70.6 us -> 21.6 us
    psum x1 -> x0, blocking collectives: 70.6 us -> none  [on_device(): lax.psum(short_terms.astype(jnp.bfloat16), 'ctx').astype(jnp.float32)]
    all_gather x0 -> x1, blocking collectives: none -> 21.6 us  [add_all(): blocks = lax.all_gather(x, axis)]
  transfers between devices with their start and end apart: 7 -> 7, of which waited for: 5 -> 5; matrix products, arithmetic and copies ran while one was open for 29% -> 32% of each run, Pallas kernels for 0% -> 0%
where the time goes in v1:
time: 427 us; the launch traced here: 426 us
  waiting for transfers between devices  171 us (40%)
  matrix products  127 us (30%)
  other arithmetic  38.6 us (9%)
  local copies, waits for them, and re-layouts  26.4 us (6%)
  starting transfers between devices  24.4 us (6%)
  blocking collectives  21.6 us (5%)
  between operations  17.4 us (4%)
    conv_general_dilated x3, matrix products, depthwise(): lax.conv_general_dilated(signal[None], kernel[:, None, :], (1,), 'VALID',...  92.3 us
    all_to_all x1, waiting for transfers between devices, on_device(): lax.all_to_all(sent_mixin, 'ctx', split_axis=0, concat_axis=0, tiled=True)  66.2 us
    all_to_all x1, waiting for transfers between devices, on_device(): lax.all_to_all(sent_head, 'ctx', split_axis=0, concat_axis=0, tiled=True)  58 us
    all_gather x1, waiting for transfers between devices, on_device(): full_weight = lax.all_gather(out_weight, 'ctx', axis=1, tiled=True)  23.1 us
    all_gather x1, blocking collectives, add_all(): blocks = lax.all_gather(x, axis)  21.6 us
    dot_general x1, matrix products, on_device(): jnp.dot(gated_rows, full_weight, preferred_element_type=jnp.float32)  17.8 us
    dot_general x1, matrix products, on_device(): lax.dot_general(out_grad, full_weight, (((1,), (1,)), ((), ())), preferre...  16.8 us
    all_to_all x1, waiting for transfers between devices, on_device(): lax.all_to_all(sent_raw, 'ctx', split_axis=0, concat_axis=0, tiled=True)  12.3 us
  transfers between devices with their start and end apart: 7, of which 5 were waited for; matrix products, arithmetic and copies ran while one was open for 32% of the time, Pallas kernels for 0%

profile of v1, /device:TPU:24, one launch (start us, length us, event | category | flops | bytes accessed | tf_op | source)
XLA Modules:
  0.0 426.3 jit_solution(6432763313315607577)
XLA Ops:
  13.8 7.9 %all-to-all-start = ((bf16[16,3,8,1024]{3,2,1,0:T(8,128)(2,1)}), bf16[16,3,8,1024]{3,2,1,0:T(8,128)(2,1)}, u32[]{:S(2)}, u32[]{:S(2)}) async-start(bf16[16,3,8,1024]{3,2,1,0:T(8,128)(2,1)} %broadcast_multiply_fusion.2), calls=%async_computation | async-start | bytes 1572864 | tf_op jit(solution)/shard_map/all_to_all | solution.py:72
  24.1 2.7 copy-done.2
  29.4 12.3 %all-to-all-done = bf16[16,3,8,1024]{3,2,1,0:T(8,128)(2,1)} async-done(((bf16[16,3,8,1024]{3,2,1,0:T(8,128)(2,1)}), bf16[16,3,8,1024]{3,2,1,0:T(8,128)(2,1)}, u32[]{:S(2)}, u32[]{:S(2)}) %all-to-all-start) | async-done | bytes 786464 | tf_op jit(solution)/shard_map/all_to_all | solution.py:72
  41.7 4.5 %all-to-all-start.1 = ((bf16[16,128,1024]{2,1,0:T(8,128)(2,1)}), bf16[16,128,1024]{2,1,0:T(8,128)(2,1)}, u32[]{:S(2)}, u32[]{:S(2)}) async-start(bf16[16,128,1024]{2,1,0:T(8,128)(2,1)} %broadcast_multiply_fusion.1), calls=%async_computation.1 | async-start | bytes 8388608 | tf_op jit(solution)/shard_map/all_to_all | solution.py:73
  48.2 2.8 rev.19
  51.0 3.5 fusion.36
  56.0 66.2 %all-to-all-done.1 = bf16[16,128,1024]{2,1,0:T(8,128)(2,1)} async-done(((bf16[16,128,1024]{2,1,0:T(8,128)(2,1)}), bf16[16,128,1024]{2,1,0:T(8,128)(2,1)}, u32[]{:S(2)}, u32[]{:S(2)}) %all-to-all-start.1) | async-done | bytes 4194336 | tf_op jit(solution)/shard_map/all_to_all | solution.py:73
  125.8 32.3 %fusion.19 = f32[1,512,1024]{2,0,1:T(1,128)} fusion(bf16[1,639,1024]{2,1,0:T(8,128)(2,1)S(1)} %fusion.22, bf16[128,1,1024]{2,0,1:T(8,128)(2,1)S(1)} %bitcast.82), kind=kOutput, calls=%fused_computation.45 | convolution fusion | flops 134217728 | bytes 3667968 | tf_op jit(solution)/shard_map/conv_general_dilated | solution.py:25
  158.1 23.1 %all-gather.2.cloned.1.call-done = bf16[1024,8192]{1,0:T(8,128)(2,1)} async-done(((bf16[1024,512]{1,0:T(8,128)(2,1)}), bf16[1024,8192]{1,0:T(8,128)(2,1)}) %all-gather.2.cloned.1.call-update) | async-done | bytes 16777232 | tf_op jit(solution)/shard_map/all_gather | solution.py:86
  181.2 16.8 %multiply_bitcast_fusion = (f32[1,512,1024]{2,1,0:T(8,128)}, bf16[512,1024]{1,0:T(8,128)(2,1)S(1)}) fusion(f32[1,512,1024]{2,0,1:T(1,128)} %fusion.19, f32[1024]{0:T(1024)S(1)} %copy-done.20, bf16[504,1024]{1,0:T(8,128)(2,1)S(1)} %copy-done.7, bf16[8,1024]{1,0:T(8,128)(2,1)S(1)} %fusion.27, f32[3,504,1024]{2,1,0:T(8,128)} %copy-done.2, ...), kind=kOutput, calls=%fused_computation.39 | convolution fusion | flops 8595177472 | bytes 37752832 | tf_op jit(solution)/shard_map/dot_general | solution.py:95
  198.0 28.3 %fusion.15 = bf16[1,128,1024]{2,0,1:T(2,128)(2,1)S(1)} fusion(bf16[512,1,1024]{2,0,1:T(8,128)(2,1)S(1)} %bitcast.80, bf16[1,639,1024]{2,1,0:T(8,128)(2,1)} %copy-done.8), kind=kOutput, calls=%fused_computation.34 | convolution fusion | flops 134217728 | bytes 2619392 | tf_op jit(solution)/shard_map/conv_general_dilated | solution.py:25
  226.4 2.6 rev.23
  229.0 17.8 %convolution_convert_fusion = bf16[512,8192]{1,0:T(8,128)(2,1)} fusion(bf16[1024,8192]{1,0:T(8,128)(2,1)} %all-gather.2.cloned.1.call-done, f32[1,512,1024]{2,0,1:T(1,128)} %fusion.19, f32[1024]{0:T(1024)S(1)} %copy-done.20, bf16[504,1024]{1,0:T(8,128)(2,1)S(1)} %copy-done.7, bf16[8,1024]{1,0:T(8,128)(2,1)S(1)} %fusion.27, f32[3,504,1024]{2,1,0:T(8,128)} %copy-done.2, ...), kind=kOutput, calls=%fused_computation | convolution fusion | flops 8598847488 | bytes 34607104 | tf_op jit(solution)/shard_map/dot_general | solution.py:90
  246.9 2.4 broadcast_multiply_fusion
  249.3 7.8 %all-to-all-start.2 = ((bf16[16,128,1024]{2,1,0:T(8,128)(2,1)}), bf16[16,128,1024]{2,1,0:T(8,128)(2,1)}, u32[]{:S(2)}, u32[]{:S(2)}) async-start(bf16[16,128,1024]{2,1,0:T(8,128)(2,1)} %broadcast_multiply_fusion), calls=%async_computation.3 | async-start | bytes 8388608 | tf_op jit(solution)/shard_map/all_to_all | solution.py:103
  260.3 58.0 %all-to-all-done.2 = bf16[16,128,1024]{2,1,0:T(8,128)(2,1)} async-done(((bf16[16,128,1024]{2,1,0:T(8,128)(2,1)}), bf16[16,128,1024]{2,1,0:T(8,128)(2,1)}, u32[]{:S(2)}, u32[]{:S(2)}) %all-to-all-start.2) | async-done | bytes 4194336 | tf_op jit(solution)/shard_map/all_to_all | solution.py:103
  320.5 31.7 %fusion.4 = f32[1,512,1024]{2,0,1:T(1,128)S(1)} fusion(bf16[1,639,1024]{2,1,0:T(8,128)(2,1)S(1)} %fusion.21, bf16[128,1,1024]{2,0,1:T(8,128)(2,1)S(1)} %bitcast.83), kind=kOutput, calls=%fused_computation.20 | convolution fusion | flops 134217728 | bytes 3667968 | tf_op jit(solution)/shard_map/conv_general_dilated | solution.py:25
  352.7 10.3 %rev.22 = f32[512,1024]{1,0:T(8,128)} reverse(f32[512,1024]{1,0:T(8,128)S(1)} %bitcast.79), dimensions={0} | reverse | bytes 4194304 | tf_op jit(solution)/shard_map/jit(_flip)/rev | solution.py:108
  363.0 3.9 fusion.9
  369.8 4.0 all-to-all-start.3
  375.6 10.8 %all-to-all-done.3 = bf16[16,3,8,1024]{3,2,1,0:T(8,128)(2,1)S(1)} async-done(((bf16[16,3,8,1024]{3,2,1,0:T(8,128)(2,1)}), bf16[16,3,8,1024]{3,2,1,0:T(8,128)(2,1)S(1)}, u32[]{:S(2)}, u32[]{:S(2)}) %all-to-all-start.3) | async-done | bytes 786464 | tf_op jit(solution)/shard_map/all_to_all | solution.py:112
  387.1 2.8 pad_maximum_fusion
  391.8 5.6 %multiply_reduce_fusion.1 = (bf16[3,1024]{1,0:T(4,128)(2,1)S(1)}, bf16[3,1024]{1,0:T(4,128)(2,1)S(1)}, bf16[3,1024]{1,0:T(4,128)(2,1)S(1)}, bf16[3,512,1024]{2,1,0:T(8,128)(2,1)}) fusion(bf16[3,8,1024]{2,1,0:T(8,128)(2,1)S(1)} %copy-done.10, bf16[3,512,1024]{2,1,0:T(8,128)(2,1)S(1)} %copy-done.1, f32[1,512,1024]{2,1,0:T(8,128)S(1)} %copy-done.4, ...), kind=kLoop, calls=%fused_computation.11 | loop fusion | flops 36166656 | bytes 25270272 | tf_op jit(solution)/shard_map/reduce_sum | solution.py:125
  397.4 21.6 %all_gather.8 = bf16[16,3,3,1024]{3,2,1,0:T(4,128)(2,1)S(1)} all-gather(bf16[1,3,3,1024]{3,2,1,0:T(4,128)(2,1)S(1)} %copy.33), channel_id=1, replica_groups=mesh['ctx'=16,'tp'=8] {'ctx'}, dimensions={0}, use_global_device_ids=true | all-gather | bytes 313344 | tf_op jit(solution)/shard_map/all_gather | solution.py:11
  (86 shorter events, 29.4 us)
Async XLA Ops:
  7.2 14.7 %copy-start = (bf16[3,512,1024]{2,1,0:T(8,128)(2,1)S(1)}, bf16[3,512,1024]{2,1,0:T(8,128)(2,1)}, u32[]{:S(2)}) copy-start(bf16[3,512,1024]{2,1,0:T(8,128)(2,1)} %param.7) | copy-start | bytes 9437188
  7.2 14.5 %copy-start.19 = (f32[3,3,1024]{2,1,0:T(4,128)S(1)}, f32[3,3,1024]{2,1,0:T(4,128)}, u32[]{:S(2)}) copy-start(f32[3,3,1024]{2,1,0:T(4,128)} %param.8) | copy-start | bytes 110596
  7.2 174.1 %all-gather.2.cloned.1.call-start = ((), (), s32[]{:S(2)}) async-start(), calls=%async_computation.5 | async-start | bytes 17825792 | tf_op jit(solution)/shard_map/all_gather | solution.py:86
  13.8 28.0 %all-to-all-start = ((bf16[16,3,8,1024]{3,2,1,0:T(8,128)(2,1)}), bf16[16,3,8,1024]{3,2,1,0:T(8,128)(2,1)}, u32[]{:S(2)}, u32[]{:S(2)}) async-start(bf16[16,3,8,1024]{3,2,1,0:T(8,128)(2,1)} %broadcast_multiply_fusion.2), calls=%async_computation | async-start | bytes 1572864 | tf_op jit(solution)/shard_map/all_to_all | solution.py:72
  21.8 33.6 %copy-start.13 = (f32[3,1,1024]{2,0,1:T(4,128)}, f32[3,1,1024]{2,0,1:T(4,128)S(1)}, u32[]{:S(2)}) copy-start(f32[3,1,1024]{2,0,1:T(4,128)S(1)} %copy.65) | copy-start | bytes 36868
  21.8 33.5 %copy-start.15 = (f32[3,1024]{1,0:T(4,128)}, f32[3,1024]{1,0:T(4,128)S(1)}, u32[]{:S(2)}) copy-start(f32[3,1024]{1,0:T(4,128)S(1)} %get-tuple-element.17) | copy-start | bytes 36868
  21.8 33.5 %copy-start.17 = (f32[3,1024]{1,0:T(4,128)}, f32[3,1024]{1,0:T(4,128)S(1)}, u32[]{:S(2)}) copy-start(f32[3,1024]{1,0:T(4,128)S(1)} %get-tuple-element.18) | copy-start | bytes 36868
  29.4 16.9 %copy-start.21 = (s32[16]{0:T(128)S(1)}, s32[16]{0:T(128)}, u32[]{:S(2)}) copy-start(s32[16]{0:T(128)} %param.13) | copy-start | bytes 196
  29.4 18.8 %copy-start.11 = (bf16[128,1024]{1,0:T(8,128)(2,1)S(1)}, bf16[128,1024]{1,0:T(8,128)(2,1)}, u32[]{:S(2)}) copy-start(bf16[128,1024]{1,0:T(8,128)(2,1)} %param.9) | copy-start | bytes 786436
  41.7 80.4 %all-to-all-start.1 = ((bf16[16,128,1024]{2,1,0:T(8,128)(2,1)}), bf16[16,128,1024]{2,1,0:T(8,128)(2,1)}, u32[]{:S(2)}, u32[]{:S(2)}) async-start(bf16[16,128,1024]{2,1,0:T(8,128)(2,1)} %broadcast_multiply_fusion.1), calls=%async_computation.1 | async-start | bytes 8388608 | tf_op jit(solution)/shard_map/all_to_all | solution.py:73
  46.3 327.5 %all-reduce.2.cloned.1.call-start = ((), (), s32[]{:S(2)}) async-start(), calls=%async_computation.7 | async-start | bytes 524288 | tf_op jit(solution)/shard_map/psum | solution.py:138
  55.4 70.4 %copy-start.12 = (bf16[128,1024]{1,0:T(8,128)(2,1)S(1)}, bf16[128,1024]{1,0:T(8,128)(2,1)}, u32[]{:S(2)}) copy-start(bf16[128,1024]{1,0:T(8,128)(2,1)} %rev.19) | copy-start | bytes 786436
  125.8 55.4 %copy-start.7 = (bf16[504,1024]{1,0:T(8,128)(2,1)S(1)}, bf16[504,1024]{1,0:T(8,128)(2,1)}, u32[]{:S(2)}) copy-start(bf16[504,1024]{1,0:T(8,128)(2,1)} %fusion.36) | copy-start | bytes 3096580
  125.8 55.4 %copy-start.20 = (f32[1024]{0:T(1024)S(1)}, f32[1024]{0:T(1024)}, u32[]{:S(2)}) copy-start(f32[1024]{0:T(1024)} %param.10) | copy-start | bytes 12292
  229.0 190.8 %reduce-scatter.2.cloned.1.call-start = ((), (), s32[]{:S(2)}) async-start(), calls=%async_computation.6 | async-start | bytes 9437184 | tf_op jit(solution)/shard_map/reduce_scatter | solution.py:89
  249.3 69.0 %all-to-all-start.2 = ((bf16[16,128,1024]{2,1,0:T(8,128)(2,1)}), bf16[16,128,1024]{2,1,0:T(8,128)(2,1)}, u32[]{:S(2)}, u32[]{:S(2)}) async-start(bf16[16,128,1024]{2,1,0:T(8,128)(2,1)} %broadcast_multiply_fusion), calls=%async_computation.3 | async-start | bytes 8388608 | tf_op jit(solution)/shard_map/all_to_all | solution.py:103
  363.0 4.0 copy-start.5
  369.8 16.6 %all-to-all-start.3 = ((bf16[16,3,8,1024]{3,2,1,0:T(8,128)(2,1)}), bf16[16,3,8,1024]{3,2,1,0:T(8,128)(2,1)S(1)}, u32[]{:S(2)}, u32[]{:S(2)}) async-start(bf16[16,3,8,1024]{3,2,1,0:T(8,128)(2,1)} %multiply_convert_fusion.2), calls=%async_computation.4 | async-start | bytes 1572864 | tf_op jit(solution)/shard_map/all_to_all | solution.py:112
  387.1 4.0 copy-start.4
  387.1 4.7 %copy-start.6 = (f32[1,512,1024]{2,1,0:T(8,128)S(1)}, f32[1,512,1024]{2,1,0:T(8,128)}, u32[]{:S(2)}) copy-start(f32[1,512,1024]{2,1,0:T(8,128)} %get-tuple-element.12) | copy-start | bytes 6291460
  387.1 4.6 %copy-start.10 = (bf16[3,8,1024]{2,1,0:T(8,128)(2,1)S(1)}, bf16[3,8,1024]{2,1,0:T(8,128)(2,1)}, u32[]{:S(2)}) copy-start(bf16[3,8,1024]{2,1,0:T(8,128)(2,1)} %copy-done.9) | copy-start | bytes 147460
  387.1 4.6 %copy-start.14 = (f32[3,1,1024]{2,0,1:T(4,128)S(1)}, f32[3,1,1024]{2,0,1:T(4,128)}, u32[]{:S(2)}) copy-start(f32[3,1,1024]{2,0,1:T(4,128)} %copy-done.13) | copy-start | bytes 36868
  387.1 4.6 %copy-start.16 = (f32[3,1024]{1,0:T(4,128)S(1)}, f32[3,1024]{1,0:T(4,128)}, u32[]{:S(2)}) copy-start(f32[3,1024]{1,0:T(4,128)} %copy-done.15) | copy-start | bytes 36868
  387.1 4.6 %copy-start.18 = (f32[3,1024]{1,0:T(4,128)S(1)}, f32[3,1024]{1,0:T(4,128)}, u32[]{:S(2)}) copy-start(f32[3,1024]{1,0:T(4,128)} %copy-done.17) | copy-start | bytes 36868
  (5 other events, 9.4 us)
Sparse Core Ops, SparseCore 0:
  10.1 171.0 all-gather.1
  229.1 118.2 all-reduce.1
  350.4 49.8 reduce-scatter.1
